TPU v7x, 256 devices: a whole 4x4x8 slice. The times are simulated.
256 devices in a mesh: seq: 32 (over z, x), feat: 8 (over y, core).
Axes of the slice: x: 4, y: 4, z: 8, core: 2. Of those that a mesh axis runs over, the one named last changes fastest.
Arguments:
- teacher_states: bfloat16 [4, 32768, 3584], P(None, 'seq', 'feat')
- student_states: bfloat16 [32768, 2304], P('seq'), may hold values from -6 to 6
- projection: bfloat16 [4, 2304, 3584], P(None, 'seq', 'feat'), may hold values from -0.125 to 0.125
- layer_pick: int32 [4], replicated, may hold values from 0 to 3, each once
- validity: int32 [32768], P('seq'), may hold values from 0 to 1, as said below
Outputs:
- whitened_error: bfloat16 [4, 32768, 3584], P(None, 'seq', 'feat')
- total_loss: float32 [], replicated
Inputs may be any that keep to these rules, and one draw needn't show every extreme that they name: `validity`: the positions form 2 sequences of 16384 positions each; in each sequence a prefix of 4096 positions or more is 1 and the rest is 0.
All inputs are finite; a program needn't handle non-finite values.
Results may differ from a plain program's by a relative error of at most 0.00045.
Values may be sent and summed in bfloat16 or wider, within the bound.
No kernel may reach another device: no remote copies, remote signals or barrier semaphores. Data moves between devices by JAX's collectives and lax.ppermute only.
A program may use at most 64 MiB of HBM per device.

v0:
```python
import functools
import jax
import jax.numpy as jnp
from jax import lax
from jax.sharding import Mesh
from jax.sharding import PartitionSpec as P

D = 3584
LAYERS = 4
SEQ = ("seq_0", "seq_1")
SEQ_FEAT = ("seq_0", "seq_1", "feat_0", "feat_1")
FEAT = ("feat_0", "feat_1")
epsilon = 1e-05


def all_in_one(value, axis):
    leaves = jax.tree.leaves(value)
    sequence = sorted(range(len(leaves)), key=lambda k: -leaves[k].size)
    width = (1, *leaves[sequence[0]].shape)[-1]
    lines = [
        jnp.pad(leaves[k].reshape(-1), (0, -leaves[k].size % width)).reshape(-1, width)
        for k in sequence
    ]
    both, at, found = (lax.all_gather(jnp.concatenate(lines), axis), 0, {})
    for k, line in zip(sequence, lines):
        slab = both[:, at : at + len(line)].reshape(len(both), -1)
        found[k] = slab[:, : leaves[k].size].reshape(-1, *leaves[k].shape)
        at += len(line)
    numbers = iter(range(len(leaves)))
    return jax.tree.map(lambda _: found[next(numbers)], value)


def combined_by_axis(value, axes, combine):
    for axis in axes:
        pieces = all_in_one(value, axis)
        value = jax.tree.map(lambda part: part[0], pieces)
        for k in range(1, lax.axis_size(axis)):
            value = combine(value, jax.tree.map(lambda part: part[k], pieces))
    return value


def over_axes(value, axes):
    return functools.reduce(lax.psum, axes, value)


def combine_moments(former, latter):
    first_count, first_mean, first_spread = former
    second_count, second_mean, second_spread = latter
    joined = first_count + second_count
    share = second_count / jnp.maximum(joined, 1.0)
    delta = second_mean - first_mean
    return (
        joined,
        first_mean + delta * share,
        first_spread + second_spread + delta * delta * first_count * share,
    )


def shards(teacher_states, student_states, projection, layer_pick, validity):
    all_weights = lax.all_gather(projection, SEQ, axis=1, tiled=True)
    weighting = validity.astype(jnp.float32)
    local_count = jnp.sum(weighting)
    chosen = jnp.take(teacher_states, layer_pick, axis=0).astype(jnp.float32)
    masked = weighting[None, :, None]
    local_sums = jnp.sum(chosen * masked, axis=1)
    local_mean = local_sums / jnp.maximum(local_count, 1.0)
    local_centred = chosen - local_mean[:, None, :]
    local_spread = jnp.sum(masked * local_centred * local_centred, axis=1)
    counted, average, spread = combined_by_axis(
        (local_count, local_mean, local_spread), SEQ, combine_moments
    )
    variance = spread / counted
    centred = chosen - average[:, None, :]
    target = centred / jnp.sqrt(variance + epsilon)[:, None, :]
    predicted = jnp.einsum(
        "tr,lrd->ltd", student_states, all_weights, preferred_element_type=jnp.float32
    )
    residual = predicted - target
    whitened_error = (masked * residual).astype(jnp.bfloat16)
    partial_value = jnp.sum(masked * residual * residual)
    squared_total = over_axes(partial_value, SEQ_FEAT)
    total_loss = squared_total / (counted * D * LAYERS)
    return (whitened_error, total_loss)


def solution(mesh):
    torus = Mesh(mesh.devices.reshape(8, 4, 4, 2), ("seq_0", "seq_1", "feat_0", "feat_1"))
    in_specs = (P(None, SEQ, FEAT), P(SEQ, None), P(None, SEQ, FEAT), P(), P(SEQ))
    out_specs = (P(None, SEQ, FEAT), P())
    return jax.shard_map(
        shards, mesh=torus, in_specs=in_specs, out_specs=out_specs, check_vma=False
    )
```

profile of v0, /device:TPU:1, one launch (start us, length us, event | category | flops | bytes accessed | tf_op | source)
XLA Modules:
  0.0 185.9 jit_solution(15718595818975984317)
XLA Ops:
  7.2 0.0 copy-start.1
  7.2 0.0 copy-start.2
  7.2 0.0 all-gather.6.cloned.1.call-start
  7.2 0.7 all-gather.6.cloned.1.call-update
  7.9 0.7 convert_element_type.12
  8.6 0.7 compare_select_fusion
  9.3 4.7 %gather_fusion = bf16[4,1024,448]{1,2,0:T(8,128)(2,1)} fusion(bf16[4,1024,448]{1,2,0:T(8,128)(2,1)} %param.5, s32[1024]{0:T(1024)S(1)} %pad_clamp_fusion), kind=kCustom, calls=%fused_computation | custom fusion | bytes 7340048 | tf_op jit(solution)/shard_map/jit(_take)/gather | solution.py:63
  13.9 0.0 copy-done.1
  13.9 0.6 convert_reduce_fusion
  15.2 0.0 copy-start
  15.2 0.8 pad.7
  16.0 0.0 copy-done.2
  16.0 3.3 %fusion.1 = f32[4,448]{1,0:T(4,128)S(1)} fusion(f32[1024]{0:T(1024)S(1)} %convert_element_type.12, bf16[4,1024,448]{1,2,0:T(8,128)(2,1)} %gather_fusion, pred[4]{0:T(512)(128)(4,1)S(1)} %compare_and_fusion), kind=kLoop, calls=%fused_computation.8 | loop fusion | flops 7338240 | bytes 3681284 | tf_op jit(solution)/shard_map/reduce_sum | solution.py:65
  19.4 0.0 copy-done
  19.4 1.8 fusion.4
  21.2 24.3 %all-gather.2 = f32[8,9,448]{2,1,0:T(8,128)S(1)} all-gather(f32[1,9,448]{2,1,0:T(8,128)S(1)} %maximum_bitcast_fusion), channel_id=2, replica_groups=mesh['seq_0'=8,'seq_1'=4,'feat_0'=4,'feat_1'=2] {'seq_0'}, dimensions={0}, use_global_device_ids=true | all-gather | bytes 145152 | tf_op jit(solution)/shard_map/all_gather | solution.py:24
  45.6 0.6 fusion.40
  55.8 0.7 fusion.20
  56.5 9.7 %all-gather.3 = f32[4,9,448]{2,1,0:T(8,128)S(1)} all-gather(f32[1,9,448]{2,1,0:T(8,128)S(1)} %maximum_bitcast_fusion.1), channel_id=3, replica_groups=mesh['seq_0'=8,'seq_1'=4,'feat_0'=4,'feat_1'=2] {'seq_1'}, dimensions={0}, use_global_device_ids=true | all-gather | bytes 80640 | tf_op jit(solution)/shard_map/all_gather | solution.py:24
  66.2 0.6 fusion.41
  71.3 0.7 multiply_add_fusion
  72.0 46.2 %all-gather.6.cloned.1.call-done = bf16[4,2304,448]{2,1,0:T(8,128)(2,1)} async-done(((bf16[4,72,448]{2,1,0:T(8,128)(2,1)}), bf16[4,2304,448]{2,1,0:T(8,128)(2,1)}) %all-gather.6.cloned.1.call-update) | async-done | bytes 8257552 | tf_op jit(solution)/shard_map/all_gather | solution.py:60
  118.2 19.1 %fusion = (f32[]{:T(128)}, bf16[4,1024,448]{1,2,0:T(8,128)(2,1)}) fusion(f32[1024]{0:T(1024)S(1)} %convert_element_type.12, f32[4,448]{1,0:T(4,128)S(1)} %get-tuple-element.7, f32[4,448]{1,0:T(4,128)S(1)} %get-tuple-element.6, bf16[4,1024,448]{1,2,0:T(8,128)(2,1)} %gather_fusion, pred[4]{0:T(512)(128)(4,1)S(1)} %compare_and_fusion, ...), kind=kOutput, calls=%fused_computation.7 | convolution fusion | flops 8472231936 | bytes 20334600 | tf_op jit(solution)/shard_map/tr,lrd->ltd/dot_general | solution.py:75
  137.3 13.0 %psum.28 = f32[]{:T(128)} all-reduce(f32[]{:T(128)} %get-tuple-element.4), channel_id=1, replica_groups=mesh['seq_0'=8,'seq_1'=4,'feat_0'=4,'feat_1'=2] {'seq_0'}, use_global_device_ids=true, to_apply=%region_4.5 | all-reduce | flops 1 | bytes 8 | tf_op jit(solution)/shard_map/psum | solution.py:43
  150.3 6.6 %psum.29 = f32[]{:T(128)} all-reduce(f32[]{:T(128)} %psum.28), channel_id=1, replica_groups=mesh['seq_0'=8,'seq_1'=4,'feat_0'=4,'feat_1'=2] {'seq_1'}, use_global_device_ids=true, to_apply=%region_5.6 | all-reduce | flops 1 | bytes 8 | tf_op jit(solution)/shard_map/psum | solution.py:43
  156.9 8.8 %psum.30 = f32[]{:T(128)} all-reduce(f32[]{:T(128)} %psum.29), channel_id=1, replica_groups=mesh['seq_0'=8,'seq_1'=4,'feat_0'=4,'feat_1'=2] {'feat_0'}, use_global_device_ids=true, to_apply=%region_6.7 | all-reduce | flops 1 | bytes 8 | tf_op jit(solution)/shard_map/psum | solution.py:43
  165.7 11.6 %psum.31 = f32[]{:T(128)} all-reduce(f32[]{:T(128)} %psum.30), channel_id=1, replica_groups=mesh['seq_0'=8,'seq_1'=4,'feat_0'=4,'feat_1'=2] {'feat_1'}, use_global_device_ids=true, to_apply=%region_7.8 | all-reduce | flops 1 | bytes 8 | tf_op jit(solution)/shard_map/psum | solution.py:43
  (11 shorter events, 0.1 us)
Async XLA Ops:
  7.2 6.8 %copy-start.1 = (s32[1024]{0:T(1024)S(1)}, s32[1024]{0:T(1024)}, u32[]{:S(2)}) copy-start(s32[1024]{0:T(1024)} %param.9) | copy-start | bytes 12292
  7.2 8.8 %copy-start.2 = (s32[4]{0:T(128)S(1)}, s32[4]{0:T(128)}, u32[]{:S(2)}) copy-start(s32[4]{0:T(128)} %param.8) | copy-start | bytes 52
  7.2 111.0 %all-gather.6.cloned.1.call-start = ((), (), s32[]{:S(2)}) async-start(), calls=%async_computation | async-start | bytes 9732096 | tf_op jit(solution)/shard_map/all_gather | solution.py:60
  15.2 4.2 %copy-start = (bf16[4,1024,448]{1,2,0:T(8,128)(2,1)S(1)}, bf16[4,1024,448]{1,2,0:T(8,128)(2,1)}, u32[]{:S(2)}) copy-start(bf16[4,1024,448]{1,2,0:T(8,128)(2,1)} %gather_fusion) | copy-start | bytes 11010052
Sparse Core Ops, SparseCore 0:
  10.6 107.5 all-gather.5
where the time goes:
time: 186 us
  blocking collectives  74.1 us (40%)
  waiting for transfers between devices  46.9 us (25%)
  between operations  30.6 us (16%)
  matrix products  19.1 us (10%)
  other arithmetic  8.52 us (5%)
  local copies, waits for them, and re-layouts  6.71 us (4%)
    all_gather x1, waiting for transfers between devices, shards(): all_weights = lax.all_gather(projection, SEQ, axis=1, tiled=True)  46.2 us
    psum x4, blocking collectives, over_axes(): return functools.reduce(lax.psum, axes, value)  40 us
    all_gather x2, blocking collectives, all_in_one(): both, at, found = (lax.all_gather(jnp.concatenate(lines), axis), 0, {})  34 us
    dot_general x1, matrix products, shards(): jnp.einsum('tr,lrd->ltd', student_states, all_weights, preferred_element_...  19.1 us
    gather x1, local copies, waits for them, and re-layouts, shards(): chosen = jnp.take(teacher_states, layer_pick, axis=0).astype(jnp.float32)  4.65 us
  transfers between devices with their start and end apart: 1, of which 1 were waited for; matrix products, arithmetic and copies ran while one was open for 8% of the time, Pallas kernels for 0%

commit v1 on v0

--- a/solution.py
+++ b/solution.py
@@ -57,7 +57,9 @@
 
 
 def shards(teacher_states, student_states, projection, layer_pick, validity):
-    all_weights = lax.all_gather(projection, SEQ, axis=1, tiled=True)
+    all_weights = jnp.concatenate(
+        lax.all_to_all(jnp.stack([projection] * lax.axis_size(SEQ)), SEQ, 0, 0), axis=1
+    )
     weighting = validity.astype(jnp.float32)
     local_count = jnp.sum(weighting)
     chosen = jnp.take(teacher_states, layer_pick, axis=0).astype(jnp.float32)

time: 186 us -> 360 us (1.94)
  blocking collectives: 74.1 us -> 282 us
  waiting for transfers between devices: 46.9 us -> 0.01 us
  between operations: 30.6 us -> 16.8 us
  local copies, waits for them, and re-layouts: 6.71 us -> 20.5 us
  starting transfers between devices: 0.04 us -> 12.1 us
    all_gather x2, blocking collectives: 34 us -> 232 us  [all_in_one(): both, at, found = (lax.all_gather(jnp.concatenate(lines), axis), 0, {})]
    all_gather x1 -> x0, waiting for transfers between devices: 46.2 us -> none  [shards(): all_weights = lax.all_gather(projection, SEQ, axis=1, tiled=True)]
    all_to_all x0 -> x1, starting transfers between devices: none -> 12.1 us  [shards(): lax.all_to_all(jnp.stack([projection] * lax.axis_size(SEQ)), SEQ, 0, 0)]
    psum x4, blocking collectives: 40 us -> 49.6 us  [over_axes(): return functools.reduce(lax.psum, axes, value)]
    reshape x0 -> x1, local copies, waits for them, and re-layouts: none -> 8.23 us  [shards(): jnp.concatenate(lax.all_to_all(jnp.stack([projection] * lax.axis_size(SEQ...]
    another operation x0 -> x1, local copies, waits for them, and re-layouts: none -> 5.72 us  [shards(): jnp.stack([projection] * lax.axis_size(SEQ))]
  transfers between devices with their start and end apart: 1 -> 1, of which waited for: 1 -> 0; matrix products, arithmetic and copies ran while one was open for 8% -> 4% of each run, Pallas kernels for 0% -> 0%
where the time goes in v1:
time: 360 us; the launch traced here: 359 us
  blocking collectives  282 us (78%)
  local copies, waits for them, and re-layouts  20.5 us (6%)
  matrix products  19.1 us (5%)
  between operations  16.8 us (5%)
  starting transfers between devices  12.1 us (3%)
  other arithmetic  8.43 us (2%)
    all_gather x2, blocking collectives, all_in_one(): both, at, found = (lax.all_gather(jnp.concatenate(lines), axis), 0, {})  232 us
    psum x4, blocking collectives, over_axes(): return functools.reduce(lax.psum, axes, value)  49.6 us
    dot_general x1, matrix products, shards(): jnp.einsum('tr,lrd->ltd', student_states, all_weights, preferred_element_...  19.1 us
    all_to_all x1, starting transfers between devices, shards(): lax.all_to_all(jnp.stack([projection] * lax.axis_size(SEQ)), SEQ, 0, 0)  12.1 us
    reshape x1, local copies, waits for them, and re-layouts, shards(): jnp.concatenate(lax.all_to_all(jnp.stack([projection] * lax.axis_size(SEQ...  8.23 us
  transfers between devices with their start and end apart: 1, of which 0 were waited for; matrix products, arithmetic and copies ran while one was open for 4% of the time, Pallas kernels for 0%

profile of v1, /device:TPU:1, one launch (start us, length us, event | category | flops | bytes accessed | tf_op | source)
XLA Modules:
  0.0 358.9 jit_solution(16790951285787530610)
XLA Ops:
  0.6 5.7 %stack.2 = bf16[32,4,72,448]{3,2,1,0:T(8,128)(2,1)} broadcast(bf16[4,72,448]{2,1,0:T(8,128)(2,1)} %param.7), dimensions={1,2,3} | broadcast | bytes 8515584 | tf_op jit(solution)/shard_map/stack | solution.py:61
  6.3 0.0 copy-start
  6.3 0.0 copy-start.1
  6.3 12.1 %all-to-all-start = ((bf16[32,4,72,448]{3,2,1,0:T(8,128)(2,1)}), bf16[32,4,72,448]{3,2,1,0:T(8,128)(2,1)}, u32[]{:S(2)}, u32[]{:S(2)}) async-start(bf16[32,4,72,448]{3,2,1,0:T(8,128)(2,1)} %stack.2), calls=%async_computation | async-start | bytes 18874368 | tf_op jit(solution)/shard_map/all_to_all | solution.py:61
  18.5 0.0 copy-done
  18.5 0.6 convert_reduce_fusion
  19.7 0.7 pad.7
  20.4 0.0 copy-done.1
  20.4 4.7 %gather_fusion = bf16[4,1024,448]{1,2,0:T(8,128)(2,1)} fusion(bf16[4,1024,448]{1,2,0:T(8,128)(2,1)} %param.5, s32[1024]{0:T(1024)S(1)} %pad_clamp_fusion), kind=kCustom, calls=%fused_computation | custom fusion | bytes 7340048 | tf_op jit(solution)/shard_map/jit(_take)/gather | solution.py:65
  25.1 3.1 fusion.1
  28.2 3.3 fusion.4
  31.6 212.5 %all-gather.2 = f32[8,9,448]{2,1,0:T(8,128)S(1)} all-gather(f32[1,9,448]{2,1,0:T(8,128)S(1)} %maximum_bitcast_fusion), channel_id=2, replica_groups=mesh['seq_0'=8,'seq_1'=4,'feat_0'=4,'feat_1'=2] {'seq_0'}, dimensions={0}, use_global_device_ids=true | all-gather | bytes 145152 | tf_op jit(solution)/shard_map/all_gather | solution.py:24
  244.1 0.6 fusion.40
  254.2 0.7 fusion.20
  254.9 19.8 %all-gather.3 = f32[4,9,448]{2,1,0:T(8,128)S(1)} all-gather(f32[1,9,448]{2,1,0:T(8,128)S(1)} %maximum_bitcast_fusion.1), channel_id=3, replica_groups=mesh['seq_0'=8,'seq_1'=4,'feat_0'=4,'feat_1'=2] {'seq_1'}, dimensions={0}, use_global_device_ids=true | all-gather | bytes 80640 | tf_op jit(solution)/shard_map/all_gather | solution.py:24
  274.7 0.6 fusion.41
  279.5 0.6 multiply_add_fusion
  280.2 0.0 all-to-all-done
  280.2 8.2 %copy.9 = bf16[4,32,72,448]{3,2,1,0:T(8,128)(2,1)} copy(bf16[4,32,72,448]{3,2,0,1:T(8,128)(2,1)} %bitcast) | data formatting | bytes 16515072 | tf_op jit(solution)/shard_map/reshape | solution.py:60
  288.4 19.1 %fusion = (f32[]{:T(128)}, bf16[4,1024,448]{1,2,0:T(8,128)(2,1)}) fusion(f32[1024]{0:T(1024)S(1)} %convert_element_type.12, f32[4,448]{1,0:T(4,128)S(1)} %get-tuple-element.7, f32[4,448]{1,0:T(4,128)S(1)} %get-tuple-element.6, bf16[4,1024,448]{1,2,0:T(8,128)(2,1)} %gather_fusion, pred[4]{0:T(512)(128)(4,1)S(1)} %compare_and_fusion, ...), kind=kOutput, calls=%fused_computation.7 | convolution fusion | flops 8472231936 | bytes 20334600 | tf_op jit(solution)/shard_map/tr,lrd->ltd/dot_general | solution.py:77
  307.5 11.3 %psum.28 = f32[]{:T(128)} all-reduce(f32[]{:T(128)} %get-tuple-element.4), channel_id=1, replica_groups=mesh['seq_0'=8,'seq_1'=4,'feat_0'=4,'feat_1'=2] {'seq_0'}, use_global_device_ids=true, to_apply=%region_4.5 | all-reduce | flops 1 | bytes 8 | tf_op jit(solution)/shard_map/psum | solution.py:43
  318.8 9.3 %psum.29 = f32[]{:T(128)} all-reduce(f32[]{:T(128)} %psum.28), channel_id=1, replica_groups=mesh['seq_0'=8,'seq_1'=4,'feat_0'=4,'feat_1'=2] {'seq_1'}, use_global_device_ids=true, to_apply=%region_5.6 | all-reduce | flops 1 | bytes 8 | tf_op jit(solution)/shard_map/psum | solution.py:43
  328.0 9.3 %psum.30 = f32[]{:T(128)} all-reduce(f32[]{:T(128)} %psum.29), channel_id=1, replica_groups=mesh['seq_0'=8,'seq_1'=4,'feat_0'=4,'feat_1'=2] {'feat_0'}, use_global_device_ids=true, to_apply=%region_6.7 | all-reduce | flops 1 | bytes 8 | tf_op jit(solution)/shard_map/psum | solution.py:43
  337.4 19.7 %psum.31 = f32[]{:T(128)} all-reduce(f32[]{:T(128)} %psum.30), channel_id=1, replica_groups=mesh['seq_0'=8,'seq_1'=4,'feat_0'=4,'feat_1'=2] {'feat_1'}, use_global_device_ids=true, to_apply=%region_7.8 | all-reduce | flops 1 | bytes 8 | tf_op jit(solution)/shard_map/psum | solution.py:43
  (13 shorter events, 0.1 us)
Async XLA Ops:
  6.3 12.1 %copy-start = (s32[1024]{0:T(1024)S(1)}, s32[1024]{0:T(1024)}, u32[]{:S(2)}) copy-start(s32[1024]{0:T(1024)} %param.9) | copy-start | bytes 12292
  6.3 14.1 %copy-start.1 = (s32[4]{0:T(128)S(1)}, s32[4]{0:T(128)}, u32[]{:S(2)}) copy-start(s32[4]{0:T(128)} %param.8) | copy-start | bytes 52
  6.3 273.8 %all-to-all-start = ((bf16[32,4,72,448]{3,2,1,0:T(8,128)(2,1)}), bf16[32,4,72,448]{3,2,1,0:T(8,128)(2,1)}, u32[]{:S(2)}, u32[]{:S(2)}) async-start(bf16[32,4,72,448]{3,2,1,0:T(8,128)(2,1)} %stack.2), calls=%async_computation | async-start | bytes 18874368 | tf_op jit(solution)/shard_map/all_to_all | solution.py:61
